TPU v7x, 256 devices: a whole 4x4x8 slice. The times are simulated.
256 devices in a mesh: strip: 64 (over z, x, core), frame: 4 (over y).
Axes of the slice: x: 4, y: 4, z: 8, core: 2. Of those that a mesh axis runs over, the one named last changes fastest.
Arguments:
- frames_in: bfloat16 [4, 256, 240, 768], P('frame', 'strip'), may hold values from -6 to 6
- dw_weight: float32 [7, 7, 768], replicated, may hold values from -0.875 to 0.875
- dw_bias: float32 [768], replicated, may hold values from -4 to 4
- ln_gain: float32 [768], replicated, may hold values from 0.5 to 2
- ln_bias: float32 [768], replicated, may hold values from -3 to 3
- w_in: bfloat16 [768, 3072], replicated, may hold values from -0.21875 to 0.21875
- b_in: float32 [3072], replicated, may hold values from -3 to 3
- w_out: bfloat16 [3072, 768], replicated, may hold values from -0.109375 to 0.109375
- b_out: float32 [768], replicated, may hold values from -3 to 3
- layer_scale: float32 [768], replicated, may hold values from 0.3 to 1.5
- depth_bins: int32 [4, 256, 240], P('frame', 'strip'), may hold values from -1 to 111, as said below
- return_counts: int32 [4, 256, 240], P('frame', 'strip'), may hold values from 1 to 4
Outputs:
- features: bfloat16 [4, 256, 240, 768], P('frame', 'strip')
- probe_stat: float32 [768, 112], replicated
Inputs may be any that keep to these rules, and one draw needn't show every extreme that they name: `depth_bins`: every row of every frame has at least one pixel with a return.
All inputs are finite; a program needn't handle non-finite values.
Results may differ from a plain program's by a relative error of at most 0.0056.
Values may be sent and summed in bfloat16 or wider, within the bound.
No kernel may reach another device: no remote copies, remote signals or barrier semaphores. Data moves between devices by JAX's collectives and lax.ppermute only.
A program may use at most 128 MiB of HBM per device.

v0:
```python
import jax
import jax.numpy as jnp
from jax import lax
from jax.sharding import PartitionSpec as P

BINS = 112
ridge = 0.05


def with_halo(cells, sides, width):
    for axis, dim in sides:
        count = lax.axis_size(axis)
        ends = count - 1
        head = lax.slice_in_dim(cells, 0, width, axis=dim)
        tail = lax.slice_in_dim(cells, cells.shape[dim] - width, cells.shape[dim], axis=dim)
        cells = jnp.concatenate(
            [
                lax.ppermute(tail, axis, [(i, (i + 1) % count) for i in range(ends)]),
                cells,
                lax.ppermute(head, axis, [((i + 1) % count, i) for i in range(ends)]),
            ],
            axis=dim,
        )
    return cells


def depthwise(padded, dw_weight, dw_bias, rows, cols):
    acc = jnp.zeros(padded.shape[:-3] + (rows, cols, padded.shape[-1]), jnp.float32) + dw_bias
    for a in range(7):
        for b in range(7):
            acc = (
                acc
                + padded[..., a : a + rows, b : b + cols, :].astype(jnp.float32) * dw_weight[a, b]
            )
    return acc


def block_tail(frame, conv, ln_gain, ln_bias, w_in, b_in, w_out, b_out, layer_scale):
    chans = frame.shape[-1]
    mean = jnp.mean(conv, axis=-1, keepdims=True)
    centered = conv - mean
    var = jnp.mean(centered * centered, axis=-1, keepdims=True)
    normed = (centered * lax.rsqrt(var + 1e-06) * ln_gain + ln_bias).astype(jnp.bfloat16)
    flat = normed.reshape(-1, chans)
    hidden = jax.nn.gelu(
        jnp.dot(flat, w_in, preferred_element_type=jnp.float32) + b_in, approximate=False
    ).astype(jnp.bfloat16)
    branch = jnp.dot(hidden, w_out, preferred_element_type=jnp.float32) + b_out
    merged = frame.reshape(-1, chans).astype(jnp.float32) + layer_scale * branch
    return merged.astype(jnp.bfloat16).reshape(frame.shape)


def cross_rows(left, right):
    return lax.dot_general(
        left, right, (((0,), (0,)), ((), ())), preferred_element_type=jnp.float32
    )


def per_device(
    frames_in,
    dw_weight,
    dw_bias,
    ln_gain,
    ln_bias,
    w_in,
    b_in,
    w_out,
    b_out,
    layer_scale,
    depth_bins,
    return_counts,
):
    rows = frames_in.shape[1]
    cols = frames_in.shape[2]
    chans = frames_in.shape[3]
    extended = with_halo(frames_in, (("strip", 1),), 3)
    extended = jnp.pad(extended, ((0, 0), (0, 0), (3, 3), (0, 0)))
    conv = depthwise(extended, dw_weight, dw_bias, rows, cols)
    features = block_tail(frames_in, conv, ln_gain, ln_bias, w_in, b_in, w_out, b_out, layer_scale)
    flat = features.reshape(-1, chans)
    bins_flat = depth_bins.reshape(-1)
    weight_int = jnp.where(bins_flat >= 0, return_counts.reshape(-1), 0)
    odd_weight = weight_int % 2
    even_weight = weight_int - odd_weight
    odd_rows = flat * odd_weight.astype(jnp.bfloat16)[:, None]
    even_rows = flat * even_weight.astype(jnp.bfloat16)[:, None]
    local_xx = cross_rows(odd_rows, flat) + cross_rows(even_rows, flat)
    matched = bins_flat[:, None] == jnp.arange(BINS, dtype=jnp.int32)[None, :]
    weighted_onehot = jnp.where(matched, weight_int[:, None], 0).astype(jnp.bfloat16)
    local_xy = cross_rows(flat, weighted_onehot)
    local_total = jnp.sum(weight_int.astype(jnp.float32))
    gram_xx, gram_xy, summed = lax.psum((local_xx, local_xy, local_total), ("strip", "frame"))
    system = gram_xx / summed + ridge * jnp.eye(chans, dtype=jnp.float32)
    lower = jnp.linalg.cholesky(system)
    probe = jax.scipy.linalg.cho_solve((lower, True), gram_xy / summed)
    return (features, probe * jnp.sqrt(summed * BINS))


def solution(mesh):
    placed = (
        P("frame", "strip", None, None),
        P(),
        P(),
        P(),
        P(),
        P(),
        P(),
        P(),
        P(),
        P(),
        P("frame", "strip", None),
        P("frame", "strip", None),
    )
    return jax.shard_map(
        per_device,
        mesh=mesh,
        in_specs=placed,
        out_specs=(P("frame", "strip", None, None), P()),
        check_vma=False,
    )
```

profile of v0, /device:TPU:99, one launch (start us, length us, event | category | flops | bytes accessed | tf_op | source)
XLA Modules:
  0.0 628.5 jit_solution(7905673559130028818)
XLA Ops:
  7.2 3.2 fusion.149
  10.4 3.7 collective-permute-start
  14.1 1.9 collective-permute-start.1
  16.7 10.1 %collective-permute-done = bf16[1,3,240,768]{3,2,1,0:T(8,128)(2,1)S(1)} collective-permute-done((bf16[1,3,240,768]{3,2,1,0:T(8,128)(2,1)}, bf16[1,3,240,768]{3,2,1,0:T(8,128)(2,1)S(1)}, u32[]{:S(2)}, u32[]{:S(2)}) %collective-permute-start) | collective-permute-done | bytes 1105952 | tf_op jit(solution)/shard_map/ppermute | solution.py:18
  27.1 4.1 collective-permute-done.1
  31.2 2.4 fusion.17
  33.5 1.3 constant_dynamic-update-slice_fusion.2
  34.9 22.8 %fusion.147 = (f32[4,240]{1,0:T(4,128)S(1)}, f32[1,4,240,768]{3,2,1,0:T(8,128)S(1)}) fusion(f32[768]{0:T(1024)S(1)} %get-tuple-element.61, bf16[1,10,246,768]{3,2,1,0:T(8,128)(2,1)S(1)} %fusion.17, f32[768]{0:T(1024)S(1)} %get-tuple-element.62, f32[768]{0:T(1024)S(1)} %get-tuple-element.15, f32[768]{0:T(1024)S(1)} %get-tuple-element.16, ...), kind=kLoop, calls=%fused_computation.295 | loop fusion | flops 109116480 | bytes 75360000 | tf_op jit(solution)/shard_map/reduce_sum | solution.py:40
  58.9 37.1 %fusion.20 = bf16[960,768]{1,0:T(8,128)(2,1)} fusion(bf16[3072,768]{1,0:T(8,128)(2,1)} %param.19, f32[3072]{0:T(1024)S(1)} %copy-done.11, bf16[960,768]{1,0:T(8,128)(2,1)S(1)} %bitcast.103, bf16[768,3072]{1,0:T(8,128)(2,1)} %param.17, f32[768]{0:T(1024)S(1)} %copy-done.12, f32[768]{0:T(1024)S(1)} %copy-done.13, bf16[1,4,240,768]{3,2,1,0:T(8,128)(2,1)S(1)} %copy-done), kind=kOutput, calls=%fused_computation.32 | convolution fusion | flops 9258024960 | bytes 13879296 | tf_op jit(solution)/shard_map/dot_general | solution.py:48
  96.1 2.9 fusion.45
  98.9 3.6 fusion.22
  102.5 3.0 fusion.28
  106.2 77.6 %psum.22 = f32[]{:T(128)} all-reduce(f32[]{:T(128)} %convert_reduce_fusion), channel_id=1, replica_groups=mesh['strip'=64,'frame'=4] {'strip','frame'}, use_global_device_ids=true, to_apply=%region_4.5 | all-reduce | flops 1 | bytes 8 | tf_op jit(solution)/shard_map/psum | solution.py:92
  184.5 191.4 %all-reduce.5.cloned.1.call-done = (f32[768,768]{0,1:T(8,128)}, f32[768,112]{0,1:T(8,128)}) async-done(((f32[768,768]{0,1:T(8,128)}, f32[768,112]{0,1:T(8,128)}), (f32[768,768]{0,1:T(8,128)}, f32[768,112]{0,1:T(8,128)})) %all-reduce.5.cloned.1.call-update) | async-done | bytes 2703376 | tf_op jit(solution)/shard_map/psum | solution.py:92
  375.9 3.9 select_add_fusion
  379.8 3.2 copy.16
  383.0 2.6 fusion.21
  385.6 1.4 copy-done.3
  387.0 11.7 %cholesky.164 = f32[128,128]{1,0:T(8,128)S(1)} custom-call(f32[128,128]{1,0:T(8,128)S(1)} %cholesky.421), custom_call_target="Cholesky" | custom-call | tf_op jit(solution)/shard_map/jit(cholesky)/cholesky | solution.py:94
  398.8 9.8 %custom-call.50 = f32[1,128,128]{1,2,0:T(8,128)S(1)} custom-call(f32[1,128,128]{2,1,0:T(8,128)S(1)} %get-tuple-element.92), custom_call_target="InvertDiagBlocksLowerTriangular" | custom-call | tf_op jit(solution)/shard_map/jit(cholesky)/cholesky | solution.py:94
  408.6 1.4 fusion.39
  410.0 1.4 convolution_subtract_fusion
  411.4 11.7 %cholesky.187 = f32[128,128]{1,0:T(8,128)S(1)} custom-call(f32[128,128]{1,0:T(8,128)S(1)} %cholesky.425), custom_call_target="Cholesky" | custom-call | tf_op jit(solution)/shard_map/jit(cholesky)/cholesky | solution.py:94
  423.5 9.9 %custom-call.51 = f32[1,128,128]{1,2,0:T(8,128)S(1)} custom-call(f32[1,128,128]{2,1,0:T(8,128)S(1)} %get-tuple-element.90), custom_call_target="InvertDiagBlocksLowerTriangular" | custom-call | tf_op jit(solution)/shard_map/jit(cholesky)/cholesky | solution.py:94
  434.1 1.9 convolution_subtract_fusion.1
  436.0 11.7 %cholesky.352 = f32[128,128]{1,0:T(8,128)S(1)} custom-call(f32[128,128]{1,0:T(8,128)S(1)} %cholesky.430), custom_call_target="Cholesky" | custom-call | tf_op jit(solution)/shard_map/jit(cholesky)/cholesky | solution.py:94
  447.9 9.8 %custom-call.52 = f32[1,128,128]{1,2,0:T(8,128)S(1)} custom-call(f32[1,128,128]{2,1,0:T(8,128)S(1)} %get-tuple-element.88), custom_call_target="InvertDiagBlocksLowerTriangular" | custom-call | tf_op jit(solution)/shard_map/jit(cholesky)/cholesky | solution.py:94
  458.1 2.1 convolution_subtract_fusion.2
  460.2 11.9 %cholesky.371 = f32[128,128]{1,0:T(8,128)S(1)} custom-call(f32[128,128]{1,0:T(8,128)S(1)} %cholesky.435), custom_call_target="Cholesky" | custom-call | tf_op jit(solution)/shard_map/jit(cholesky)/cholesky | solution.py:94
  472.3 9.8 %custom-call.53 = f32[1,128,128]{1,2,0:T(8,128)S(1)} custom-call(f32[1,128,128]{2,1,0:T(8,128)S(1)} %get-tuple-element.86), custom_call_target="InvertDiagBlocksLowerTriangular" | custom-call | tf_op jit(solution)/shard_map/jit(cholesky)/cholesky | solution.py:94
  482.4 1.9 convolution_subtract_fusion.3
  484.3 11.7 %cholesky.390 = f32[128,128]{1,0:T(8,128)S(1)} custom-call(f32[128,128]{1,0:T(8,128)S(1)} %cholesky.440), custom_call_target="Cholesky" | custom-call | tf_op jit(solution)/shard_map/jit(cholesky)/cholesky | solution.py:94
  496.2 9.8 %custom-call.54 = f32[1,128,128]{1,2,0:T(8,128)S(1)} custom-call(f32[1,128,128]{2,1,0:T(8,128)S(1)} %get-tuple-element.84), custom_call_target="InvertDiagBlocksLowerTriangular" | custom-call | tf_op jit(solution)/shard_map/jit(cholesky)/cholesky | solution.py:94
  506.3 1.8 convolution_subtract_fusion.4
  508.1 11.7 %cholesky.408 = f32[128,128]{1,0:T(8,128)S(1)} custom-call(f32[128,128]{1,0:T(8,128)S(1)} %convolution_subtract_fusion.4), custom_call_target="Cholesky" | custom-call | tf_op jit(solution)/shard_map/jit(cholesky)/cholesky | solution.py:94
  527.1 1.6 select_select_fusion
  528.7 21.1 %while.1 = (s32[]{:T(128)}, f32[768,768]{0,1:T(8,128)}, s32[6,2]{0,1:T(2,128)S(1)}, f32[6,128,128]{2,1,0:T(8,128)}, s32[]{:T(128)}) while((s32[]{:T(128)}, f32[768,768]{0,1:T(8,128)}, s32[6,2]{0,1:T(2,128)S(1)}, f32[6,128,128]{2,1,0:T(8,128)}, s32[]{:T(128)}) %tuple.86), condition=%wide.while_cond, body=%wide.while_body.sunk | while | flops 2 | bytes 393829 | solution.py:95
  529.3 2.2 dynamic-slice.7
  532.8 2.2 dynamic-slice.7
  536.3 2.2 dynamic-slice.7
  539.9 2.2 dynamic-slice.7
  543.4 2.2 dynamic-slice.7
  546.9 2.1 dynamic-slice.7
  549.8 59.9 %custom-call.55 = f32[6,128,128]{1,2,0:T(8,128)S(1)} custom-call(f32[6,128,128]{2,1,0:T(8,128)} %get-tuple-element.9), custom_call_target="InvertDiagBlocksLowerTriangular" | custom-call | tf_op jit(solution)/shard_map/jit(_cho_solve)/triangular_solve | solution.py:95
  610.6 1.0 convolution_subtract_fusion.8
  611.8 1.2 convolution_subtract_fusion.7
  613.2 1.3 convolution_subtract_fusion.12
  614.7 1.3 convolution_subtract_fusion.11
  (135 shorter events, 23.1 us)
Async XLA Ops:
  7.2 19.7 %copy-start = (bf16[1,4,240,768]{3,2,1,0:T(8,128)(2,1)S(1)}, bf16[1,4,240,768]{3,2,1,0:T(8,128)(2,1)}, u32[]{:S(2)}) copy-start(bf16[1,4,240,768]{3,2,1,0:T(8,128)(2,1)} %param.12) | copy-start | bytes 4423684
  7.2 8.9 %copy-start.7 = (s32[1,4,240]{2,1,0:T(4,128)S(1)}, s32[1,4,240]{2,1,0:T(4,128)}, u32[]{:S(2)}) copy-start(s32[1,4,240]{2,1,0:T(4,128)} %param.22) | copy-start | bytes 11524
  7.2 9.0 %copy-start.6 = (s32[1,4,240]{2,1,0:T(4,128)S(1)}, s32[1,4,240]{2,1,0:T(4,128)}, u32[]{:S(2)}) copy-start(s32[1,4,240]{2,1,0:T(4,128)} %param.23) | copy-start | bytes 11524
  7.2 9.0 %copy-start.5 = (f32[7,7,768]{2,1,0:T(8,128)S(1)}, f32[7,7,768]{2,1,0:T(8,128)}, u32[]{:S(2)}) copy-start(f32[7,7,768]{2,1,0:T(8,128)} %param.13) | copy-start | bytes 451588
  7.2 368.7 %all-reduce.5.cloned.1.call-start = ((), (), s32[]{:S(2)}) async-start(), calls=%async_computation | async-start | bytes 5406720 | tf_op jit(solution)/shard_map/psum | solution.py:92
  10.4 16.3 %collective-permute-start = (bf16[1,3,240,768]{3,2,1,0:T(8,128)(2,1)}, bf16[1,3,240,768]{3,2,1,0:T(8,128)(2,1)S(1)}, u32[]{:S(2)}, u32[]{:S(2)}) collective-permute-start(bf16[1,3,240,768]{3,2,1,0:T(8,128)(2,1)} %get-tuple-element.81), channel_id=1, source_target_pairs={{0,4},{4,8},{8,12},{12,16},{16,20},{20,24},{24,28},{28,32},{32,36}... | collective-permute-start | bytes 3317768 | tf_op jit(solution)/shard_map/ppermute | solution.py:18
  14.1 17.0 %collective-permute-start.1 = (bf16[1,3,240,768]{3,2,1,0:T(8,128)(2,1)}, bf16[1,3,240,768]{3,2,1,0:T(8,128)(2,1)}, u32[]{:S(2)}, u32[]{:S(2)}) collective-permute-start(bf16[1,3,240,768]{3,2,1,0:T(8,128)(2,1)} %get-tuple-element.82), channel_id=1, source_target_pairs={{4,0},{8,4},{12,8},{16,12},{20,16},{24,20},{28,24},{32,28},{36,32}... | collective-permute-start | bytes 3317768 | tf_op jit(solution)/shard_map/ppermute | solution.py:20
  27.1 7.8 %copy-start.8 = (f32[768]{0:T(1024)S(1)}, f32[768]{0:T(1024)}, u32[]{:S(2)}) copy-start(f32[768]{0:T(1024)} %param.14) | copy-start | bytes 9220
  57.7 0.7 copy-start.9
  57.7 0.7 copy-start.10
  58.2 0.7 copy-start.11
  58.2 0.7 copy-start.12
  58.2 0.7 copy-start.13
  98.9 3.6 copy-start.14
  379.8 3.2 copy-start.1
  385.6 1.4 copy-start.3
  527.1 82.6 %copy-start.4 = (f32[768,112]{0,1:T(8,128)S(1)}, f32[768,112]{0,1:T(8,128)}, u32[]{:S(2)}) copy-start(f32[768,112]{0,1:T(8,128)} %get-tuple-element.72) | copy-start | bytes 1032196
  549.8 66.4 %copy-start.2 = (f32[768,768]{0,1:T(8,128)S(1)}, f32[768,768]{0,1:T(8,128)}, u32[]{:S(2)}) copy-start(f32[768,768]{0,1:T(8,128)} %get-tuple-element.157) | copy-start | bytes 7077892
Sparse Core Ops, SparseCore 0:
  105.7 270.1 all-reduce.4
where the time goes:
time: 634 us; the launch traced here: 629 us
  other arithmetic  219 us (35%)
  waiting for transfers between devices  206 us (32%)
  blocking collectives  77.6 us (12%)
  matrix products  68.4 us (11%)
  local copies, waits for them, and re-layouts  32.2 us (5%)
  between operations  19.6 us (3%)
    psum x1, waiting for transfers between devices, per_device(): lax.psum((local_xx, local_xy, local_total), ('strip', 'frame'))  191 us
    another operation x22, other arithmetic, per_device(): lower = jnp.linalg.cholesky(system)  123 us
    psum x1, blocking collectives, per_device(): lax.psum((local_xx, local_xy, local_total), ('strip', 'frame'))  77.6 us
    another operation x3, other arithmetic, per_device(): probe = jax.scipy.linalg.cho_solve((lower, True), gram_xy / summed)  61.5 us
    dot_general x1, matrix products, block_tail(): branch = jnp.dot(hidden, w_out, preferred_element_type=jnp.float32) + b_out  37.1 us
    reduce_sum x1, other arithmetic, block_tail(): mean = jnp.mean(conv, axis=-1, keepdims=True)  22.8 us
    another operation x30, local copies, waits for them, and re-layouts  21 us
  transfers between devices with their start and end apart: 3, of which 3 were waited for; matrix products, arithmetic and copies ran while one was open for 0% of the time, Pallas kernels for 0%

commit v1 on v0

--- a/solution.py
+++ b/solution.py
@@ -89,7 +89,9 @@
     weighted_onehot = jnp.where(matched, weight_int[:, None], 0).astype(jnp.bfloat16)
     local_xy = cross_rows(flat, weighted_onehot)
     local_total = jnp.sum(weight_int.astype(jnp.float32))
-    gram_xx, gram_xy, summed = lax.psum((local_xx, local_xy, local_total), ("strip", "frame"))
+    gram_xx, gram_xy, summed = lax.psum(
+        lax.psum((local_xx, local_xy, local_total), "strip"), "frame"
+    )
     system = gram_xx / summed + ridge * jnp.eye(chans, dtype=jnp.float32)
     lower = jnp.linalg.cholesky(system)
     probe = jax.scipy.linalg.cho_solve((lower, True), gram_xy / summed)

time: 634 us -> 699 us (1.10)
  the two profiles are of different devices: /device:TPU:99 before, /device:TPU:0 now
where the time goes in v1:
time: 699 us; the launch traced here: 693 us
  other arithmetic  219 us (31%)
  waiting for transfers between devices  212 us (30%)
  blocking collectives  139 us (20%)
  matrix products  68.4 us (10%)
  local copies, waits for them, and re-layouts  32.1 us (5%)
  between operations  19.7 us (3%)
    psum x1, waiting for transfers between devices, per_device(): lax.psum((local_xx, local_xy, local_total), 'strip')  209 us
    psum x1, blocking collectives, per_device(): lax.psum((local_xx, local_xy, local_total), 'strip')  128 us
    another operation x22, other arithmetic, per_device(): lower = jnp.linalg.cholesky(system)  123 us
    another operation x3, other arithmetic, per_device(): probe = jax.scipy.linalg.cho_solve((lower, True), gram_xy / summed)  61.5 us
    dot_general x1, matrix products, block_tail(): branch = jnp.dot(hidden, w_out, preferred_element_type=jnp.float32) + b_out  37.1 us
    reduce_sum x1, other arithmetic, block_tail(): mean = jnp.mean(conv, axis=-1, keepdims=True)  22.8 us
    another operation x30, local copies, waits for them, and re-layouts  20.9 us
  transfers between devices with their start and end apart: 4, of which 3 were waited for; matrix products, arithmetic and copies ran while one was open for 0% of the time, Pallas kernels for 0%

profile of v1, /device:TPU:0, one launch (start us, length us, event | category | flops | bytes accessed | tf_op | source)
XLA Modules:
  0.0 693.4 jit_solution(15111667416066878239)
XLA Ops:
  7.2 3.2 fusion.149
  10.4 1.3 collective-permute-start
  11.8 1.3 collective-permute-start.1
  14.6 2.2 collective-permute-done.1
  16.8 2.4 fusion.17
  19.1 1.3 constant_dynamic-update-slice_fusion.2
  20.5 22.8 %fusion.147 = (f32[4,240]{1,0:T(4,128)S(1)}, f32[1,4,240,768]{3,2,1,0:T(8,128)S(1)}) fusion(f32[768]{0:T(1024)S(1)} %get-tuple-element.61, bf16[1,10,246,768]{3,2,1,0:T(8,128)(2,1)S(1)} %fusion.17, f32[768]{0:T(1024)S(1)} %get-tuple-element.62, f32[768]{0:T(1024)S(1)} %get-tuple-element.15, f32[768]{0:T(1024)S(1)} %get-tuple-element.16, ...), kind=kLoop, calls=%fused_computation.295 | loop fusion | flops 109116480 | bytes 75360000 | tf_op jit(solution)/shard_map/reduce_sum | solution.py:40
  44.5 37.1 %fusion.20 = bf16[960,768]{1,0:T(8,128)(2,1)} fusion(bf16[3072,768]{1,0:T(8,128)(2,1)} %param.19, f32[3072]{0:T(1024)S(1)} %copy-done.11, bf16[960,768]{1,0:T(8,128)(2,1)S(1)} %bitcast.103, bf16[768,3072]{1,0:T(8,128)(2,1)} %param.17, f32[768]{0:T(1024)S(1)} %copy-done.12, f32[768]{0:T(1024)S(1)} %copy-done.13, bf16[1,4,240,768]{3,2,1,0:T(8,128)(2,1)S(1)} %copy-done), kind=kOutput, calls=%fused_computation.32 | convolution fusion | flops 9258024960 | bytes 13879296 | tf_op jit(solution)/shard_map/dot_general | solution.py:48
  81.7 2.9 fusion.45
  84.6 3.6 fusion.22
  88.1 3.1 fusion.28
  91.3 209.0 %all-reduce.7.cloned.1.call-done = (f32[768,768]{0,1:T(8,128)}, f32[768,112]{0,1:T(8,128)}) async-done(((f32[768,768]{0,1:T(8,128)}, f32[768,112]{0,1:T(8,128)}), (f32[768,768]{0,1:T(8,128)}, f32[768,112]{0,1:T(8,128)})) %all-reduce.7.cloned.1.call-update) | async-done | bytes 2703376 | tf_op jit(solution)/shard_map/psum | solution.py:93
  300.9 128.2 %psum.44 = f32[]{:T(128)} all-reduce(f32[]{:T(128)} %convert_reduce_fusion), channel_id=1, replica_groups=mesh['strip'=64,'frame'=4] {'strip'}, use_global_device_ids=true, to_apply=%region_5.6 | all-reduce | flops 1 | bytes 8 | tf_op jit(solution)/shard_map/psum | solution.py:93
  429.0 11.1 %psum.45 = f32[]{:T(128)} all-reduce(f32[]{:T(128)} %psum.44), channel_id=1, replica_groups=mesh['strip'=64,'frame'=4] {'frame'}, use_global_device_ids=true, to_apply=%region_6.7 | all-reduce | flops 1 | bytes 8 | tf_op jit(solution)/shard_map/psum | solution.py:92
  440.9 3.9 select_add_fusion
  444.8 3.2 copy.16
  448.0 2.6 fusion.21
  450.6 1.4 copy-done.3
  452.0 11.7 %cholesky.164 = f32[128,128]{1,0:T(8,128)S(1)} custom-call(f32[128,128]{1,0:T(8,128)S(1)} %cholesky.421), custom_call_target="Cholesky" | custom-call | tf_op jit(solution)/shard_map/jit(cholesky)/cholesky | solution.py:96
  463.8 9.8 %custom-call.50 = f32[1,128,128]{1,2,0:T(8,128)S(1)} custom-call(f32[1,128,128]{2,1,0:T(8,128)S(1)} %get-tuple-element.94), custom_call_target="InvertDiagBlocksLowerTriangular" | custom-call | tf_op jit(solution)/shard_map/jit(cholesky)/cholesky | solution.py:96
  473.6 1.4 fusion.39
  475.0 1.4 convolution_subtract_fusion
  476.4 11.7 %cholesky.187 = f32[128,128]{1,0:T(8,128)S(1)} custom-call(f32[128,128]{1,0:T(8,128)S(1)} %cholesky.425), custom_call_target="Cholesky" | custom-call | tf_op jit(solution)/shard_map/jit(cholesky)/cholesky | solution.py:96
  488.5 9.9 %custom-call.51 = f32[1,128,128]{1,2,0:T(8,128)S(1)} custom-call(f32[1,128,128]{2,1,0:T(8,128)S(1)} %get-tuple-element.92), custom_call_target="InvertDiagBlocksLowerTriangular" | custom-call | tf_op jit(solution)/shard_map/jit(cholesky)/cholesky | solution.py:96
  499.1 1.9 convolution_subtract_fusion.1
  501.0 11.7 %cholesky.352 = f32[128,128]{1,0:T(8,128)S(1)} custom-call(f32[128,128]{1,0:T(8,128)S(1)} %cholesky.430), custom_call_target="Cholesky" | custom-call | tf_op jit(solution)/shard_map/jit(cholesky)/cholesky | solution.py:96
  512.9 9.8 %custom-call.52 = f32[1,128,128]{1,2,0:T(8,128)S(1)} custom-call(f32[1,128,128]{2,1,0:T(8,128)S(1)} %get-tuple-element.90), custom_call_target="InvertDiagBlocksLowerTriangular" | custom-call | tf_op jit(solution)/shard_map/jit(cholesky)/cholesky | solution.py:96
  523.1 2.1 convolution_subtract_fusion.2
  525.2 11.9 %cholesky.371 = f32[128,128]{1,0:T(8,128)S(1)} custom-call(f32[128,128]{1,0:T(8,128)S(1)} %cholesky.435), custom_call_target="Cholesky" | custom-call | tf_op jit(solution)/shard_map/jit(cholesky)/cholesky | solution.py:96
  537.3 9.8 %custom-call.53 = f32[1,128,128]{1,2,0:T(8,128)S(1)} custom-call(f32[1,128,128]{2,1,0:T(8,128)S(1)} %get-tuple-element.88), custom_call_target="InvertDiagBlocksLowerTriangular" | custom-call | tf_op jit(solution)/shard_map/jit(cholesky)/cholesky | solution.py:96
  547.4 1.9 convolution_subtract_fusion.3
  549.3 11.7 %cholesky.390 = f32[128,128]{1,0:T(8,128)S(1)} custom-call(f32[128,128]{1,0:T(8,128)S(1)} %cholesky.440), custom_call_target="Cholesky" | custom-call | tf_op jit(solution)/shard_map/jit(cholesky)/cholesky | solution.py:96
  561.2 9.8 %custom-call.54 = f32[1,128,128]{1,2,0:T(8,128)S(1)} custom-call(f32[1,128,128]{2,1,0:T(8,128)S(1)} %get-tuple-element.86), custom_call_target="InvertDiagBlocksLowerTriangular" | custom-call | tf_op jit(solution)/shard_map/jit(cholesky)/cholesky | solution.py:96
  571.3 1.8 convolution_subtract_fusion.4
  573.1 11.7 %cholesky.408 = f32[128,128]{1,0:T(8,128)S(1)} custom-call(f32[128,128]{1,0:T(8,128)S(1)} %convolution_subtract_fusion.4), custom_call_target="Cholesky" | custom-call | tf_op jit(solution)/shard_map/jit(cholesky)/cholesky | solution.py:96
  592.1 1.6 select_select_fusion
  593.7 21.0 %while.1 = (s32[]{:T(128)}, f32[768,768]{0,1:T(8,128)}, s32[6,2]{0,1:T(2,128)S(1)}, f32[6,128,128]{2,1,0:T(8,128)}, s32[]{:T(128)}) while((s32[]{:T(128)}, f32[768,768]{0,1:T(8,128)}, s32[6,2]{0,1:T(2,128)S(1)}, f32[6,128,128]{2,1,0:T(8,128)}, s32[]{:T(128)}) %tuple.86), condition=%wide.while_cond, body=%wide.while_body.sunk | while | flops 2 | bytes 393829 | solution.py:97
  594.3 2.2 dynamic-slice.7
  597.8 2.2 dynamic-slice.7
  601.3 2.2 dynamic-slice.7
  604.8 2.2 dynamic-slice.7
  608.3 2.2 dynamic-slice.7
  611.8 2.1 dynamic-slice.7
  614.6 59.9 %custom-call.55 = f32[6,128,128]{1,2,0:T(8,128)S(1)} custom-call(f32[6,128,128]{2,1,0:T(8,128)} %get-tuple-element.9), custom_call_target="InvertDiagBlocksLowerTriangular" | custom-call | tf_op jit(solution)/shard_map/jit(_cho_solve)/triangular_solve | solution.py:97
  675.5 1.0 convolution_subtract_fusion.8
  676.7 1.2 convolution_subtract_fusion.7
  678.1 1.2 convolution_subtract_fusion.12
  679.6 1.3 convolution_subtract_fusion.11
  (139 shorter events, 23.8 us)
Async XLA Ops:
  7.2 7.2 %copy-start = (bf16[1,4,240,768]{3,2,1,0:T(8,128)(2,1)S(1)}, bf16[1,4,240,768]{3,2,1,0:T(8,128)(2,1)}, u32[]{:S(2)}) copy-start(bf16[1,4,240,768]{3,2,1,0:T(8,128)(2,1)} %param.12) | copy-start | bytes 4423684
  7.2 5.9 copy-start.7
  7.2 6.0 copy-start.6
  7.2 6.1 copy-start.5
  7.2 293.1 %all-reduce.7.cloned.1.call-start = ((), (), s32[]{:S(2)}) async-start(), calls=%async_computation | async-start | bytes 5406720 | tf_op jit(solution)/shard_map/psum | solution.py:93
  10.4 3.8 collective-permute-start
  11.8 5.0 collective-permute-start.1
  14.6 5.9 copy-start.8
  43.3 0.7 copy-start.9
  43.3 0.7 copy-start.10
  43.8 0.7 copy-start.11
  43.8 0.7 copy-start.12
  43.8 0.7 copy-start.13
  84.6 3.6 copy-start.14
  91.2 349.6 %all-reduce.9.cloned.1.call-start = ((), (), s32[]{:S(2)}) async-start(), calls=%async_computation.1 | async-start | bytes 5406720 | tf_op jit(solution)/shard_map/psum | solution.py:92
  444.8 3.2 copy-start.1
  450.6 1.4 copy-start.3
  592.1 82.5 %copy-start.4 = (f32[768,112]{0,1:T(8,128)S(1)}, f32[768,112]{0,1:T(8,128)}, u32[]{:S(2)}) copy-start(f32[768,112]{0,1:T(8,128)} %get-tuple-element.74) | copy-start | bytes 1032196
  614.6 66.4 %copy-start.2 = (f32[768,768]{0,1:T(8,128)S(1)}, f32[768,768]{0,1:T(8,128)}, u32[]{:S(2)}) copy-start(f32[768,768]{0,1:T(8,128)} %get-tuple-element.163) | copy-start | bytes 7077892
Sparse Core Ops, SparseCore 0:
  91.4 208.8 all-reduce.6
  302.7 72.6 all-reduce.8
